TPU v7x, 32 devices: a whole 2x2x4 slice. The times are simulated.
32 devices in a mesh: batch: 4 (over y, core), seq: 8 (over z, x).
Axes of the slice: x: 2, y: 2, z: 4, core: 2. Of those that a mesh axis runs over, the one named last changes fastest.
Arguments:
- tokens: bfloat16 [4, 1024, 1024], P('batch', 'seq'), may hold values from -6 to 6
- w_query: bfloat16 [512, 512], replicated, may hold values from -0.25 to 0.25
- w_value: bfloat16 [512, 512], replicated, may hold values from -0.25 to 0.25
- w_out: bfloat16 [512, 512], replicated, may hold values from -0.25 to 0.25
- long_filter: float32 [512, 1024], P('seq'), may hold values from -0.1875 to 0.1875
- cotangent: bfloat16 [4, 1024, 1024], P('batch', 'seq'), may hold values from -6 to 6
Outputs:
- block_out: bfloat16 [4, 1024, 1024], P('batch', 'seq')
- grad_tokens: bfloat16 [4, 1024, 1024], P('batch', 'seq')
- grad_query: float32 [512, 512], P('seq')
- grad_value: float32 [512, 512], P('seq')
- grad_out: float32 [512, 512], P('seq')
- grad_filter: float32 [512, 1024], P('seq')
All inputs are finite; a program needn't handle non-finite values.
Results may differ from a plain program's by a relative error of at most 0.017.
Values may be sent and summed in bfloat16 or wider, within the bound.
A program may use at most 64 MiB of HBM per device.

v0:
```python
import math

import jax
import jax.numpy as jnp
from jax import lax
from jax.sharding import PartitionSpec as P

precise = lax.Precision.HIGH


def swapped(x, axis, stride):
    return lax.ppermute(x, axis, [(i, i ^ 1 << stride) for i in range(lax.axis_size(axis))])


def angle_tables(count_rows, count_cols, period):
    left = lax.broadcasted_iota(jnp.int32, (count_rows, count_cols), 0)
    right = lax.broadcasted_iota(jnp.int32, (count_rows, count_cols), 1)
    turns = left * right % period
    angle = turns.astype(jnp.float32) * (2.0 * math.pi / period)
    return (jnp.cos(angle), jnp.sin(angle))


def rotation(cosines, sines, direction):
    upper = jnp.stack([cosines, direction * sines])
    lower_row = jnp.stack([-direction * sines, cosines])
    return jnp.stack([upper, lower_row])


def split_sizes(length):
    period = 2 * length
    first = 1 << (period.bit_length() - 1 + 1) // 2
    return (first, period // first)


def make_tables(first, second):
    cos_first, sin_first = angle_tables(first, first, first)
    cos_twist, sin_twist = angle_tables(first, second, first * second)
    cos_second, sin_second = angle_tables(second, second, second)
    forward_first = rotation(cos_first, sin_first, 1.0)
    inverse_first = rotation(cos_first, sin_first, -1.0)
    forward_second = rotation(cos_second, sin_second, 1.0)
    inverse_second = rotation(cos_second, sin_second, -1.0)
    return (forward_first, inverse_first, forward_second, inverse_second, cos_twist, sin_twist)


def forward_spectrum(signal, tables, first, second):
    forward_first, inverse_first, forward_second, inverse_second, cos_twist, sin_twist = tables
    lower = first // 2
    folded = signal.reshape(2, signal.shape[1], lower, second)
    section = jnp.einsum("brnm,abnk->arkm", folded, forward_first[:, :, :lower], precision=precise)
    turned = jnp.stack(
        [
            section[0] * cos_twist + section[1] * sin_twist,
            section[1] * cos_twist - section[0] * sin_twist,
        ]
    )
    return jnp.einsum("brkm,abmj->arkj", turned, forward_second, precision=precise)


def inverse_spectrum(spectrum, tables, first, second, both):
    forward_first, inverse_first, forward_second, inverse_second, cos_twist, sin_twist = tables
    lower = first // 2
    rows = spectrum.shape[1]
    inner = jnp.einsum("brkj,abjm->arkm", spectrum, inverse_second, precision=precise)
    turned = jnp.stack(
        [inner[0] * cos_twist - inner[1] * sin_twist, inner[1] * cos_twist + inner[0] * sin_twist]
    )
    if both:
        signal = jnp.einsum(
            "brkm,abkn->arnm", turned, inverse_first[:, :, :, :lower], precision=precise
        )
        return (signal / (first * second)).reshape(2, rows, lower * second)
    signal = jnp.einsum("brkm,bkn->rnm", turned, inverse_first[0][:, :, :lower], precision=precise)
    return (signal / (first * second)).reshape(rows, lower * second)


def complex_product(left, right):
    return jnp.stack(
        [left[0] * right[0] - left[1] * right[1], left[0] * right[1] + left[1] * right[0]]
    )


def conjugate_product(left, right):
    return jnp.stack(
        [left[0] * right[0] + left[1] * right[1], left[0] * right[1] - left[1] * right[0]]
    )


def mirror(array, seq_dim):
    moved = array
    for bit_index in range(lax.axis_size("seq").bit_length() - 1):
        moved = swapped(moved, "seq", bit_index)
    return jnp.flip(moved, axis=seq_dim)


def to_channels(stacked):
    return lax.all_to_all(stacked, "seq", split_axis=1, concat_axis=2, tiled=True)


def to_tokens(stacked):
    return lax.all_to_all(stacked, "seq", split_axis=2, concat_axis=1, tiled=True)


def body(tokens, w_query, w_value, w_out, long_filter, cotangent):
    floats = jnp.float32
    halves = jnp.bfloat16
    half = w_query.shape[0]
    seq_count = lax.axis_size("seq")
    batch_count = lax.axis_size("batch")
    length = tokens.shape[1] * seq_count
    first, second = split_sizes(length)
    tables = make_tables(first, second)
    scale = (2.0 * batch_count * length) ** (-0.5)
    source = tokens[0]
    front = source[:, :half]
    back = source[:, half:]
    back_strand = mirror(back, 0)[:, ::-1]
    strands = jnp.stack([front, back_strand])
    query = jnp.einsum("stk,kh->sht", strands, w_query, preferred_element_type=floats).astype(
        halves
    )
    value = jnp.einsum("stk,kh->sht", strands, w_value, preferred_element_type=floats).astype(
        halves
    )
    value_sig = to_channels(value).astype(floats)
    value_spec = forward_spectrum(value_sig, tables, first, second)
    taps_spec = forward_spectrum(
        jnp.stack([long_filter, jnp.zeros_like(long_filter)]), tables, first, second
    )
    conv_sig = inverse_spectrum(complex_product(value_spec, taps_spec), tables, first, second, True)
    conv_tok = to_tokens(conv_sig.astype(halves))
    gated = (query.astype(floats) * conv_tok.astype(floats)).astype(halves)
    gated_back = mirror(gated[1], 1)
    out_front = jnp.einsum("ht,hk->tk", gated[0], w_out, preferred_element_type=floats)
    out_back = jnp.einsum("ht,hk->tk", gated_back, w_out, preferred_element_type=floats)
    block_out = jnp.concatenate(
        [front.astype(floats) + out_front, back.astype(floats) + out_back[:, ::-1]], axis=1
    ).astype(halves)[None]
    upstream = cotangent[0]
    up_front = upstream[:, :half]
    up_back = upstream[:, half:]
    grad_back = mirror(up_back, 0)[:, ::-1]
    grad_strands = jnp.stack([up_front, grad_back])
    grad_gated = jnp.einsum(
        "stk,hk->sht", grad_strands, w_out, preferred_element_type=floats
    ).astype(halves)
    grad_query_t = (grad_gated.astype(floats) * conv_tok.astype(floats)).astype(halves)
    grad_conv = (grad_gated.astype(floats) * query.astype(floats)).astype(halves)
    grad_sig = to_channels(grad_conv).astype(floats)
    grad_spec = forward_spectrum(grad_sig, tables, first, second)
    value_grad_sig = inverse_spectrum(
        conjugate_product(taps_spec, grad_spec), tables, first, second, True
    )
    filter_part = (
        inverse_spectrum(conjugate_product(value_spec, grad_spec), tables, first, second, False)
        * scale
    )
    grad_value_t = to_tokens(value_grad_sig.astype(halves))
    front_in = jnp.einsum(
        "ht,kh->tk", grad_query_t[0], w_query, preferred_element_type=floats
    ) + jnp.einsum("ht,kh->tk", grad_value_t[0], w_value, preferred_element_type=floats)
    paired = jnp.stack([grad_query_t[1], grad_value_t[1]])
    paired = mirror(paired, 2)
    back_in = jnp.einsum(
        "ht,kh->tk", paired[0], w_query, preferred_element_type=floats
    ) + jnp.einsum("ht,kh->tk", paired[1], w_value, preferred_element_type=floats)
    grad_tokens = jnp.concatenate(
        [up_front.astype(floats) + front_in, up_back.astype(floats) + back_in[:, ::-1]], axis=1
    ).astype(halves)[None]
    term_query = jnp.einsum("stk,sht->kh", strands, grad_query_t, preferred_element_type=floats)
    term_value = jnp.einsum("stk,sht->kh", strands, grad_value_t, preferred_element_type=floats)
    term_out = jnp.einsum("sht,stk->hk", gated, grad_strands, preferred_element_type=floats)
    share = lax.psum_scatter(
        jnp.concatenate([term_query, term_value, term_out], axis=1) * scale,
        "seq",
        scatter_dimension=0,
        tiled=True,
    )
    share, filter_total = (
        lax.psum(share.astype(jnp.bfloat16), "batch").astype(jnp.float32),
        lax.psum(filter_part.astype(jnp.bfloat16), "batch").astype(jnp.float32),
    )
    return (
        block_out,
        grad_tokens,
        share[:, :half],
        share[:, half : 2 * half],
        share[:, 2 * half :],
        filter_total,
    )


def solution(mesh):
    in_specs = (P("batch", "seq", None), P(), P(), P(), P("seq", None), P("batch", "seq", None))
    out_specs = (
        P("batch", "seq", None),
        P("batch", "seq", None),
        P("seq", None),
        P("seq", None),
        P("seq", None),
        P("seq", None),
    )
    return jax.shard_map(body, mesh=mesh, in_specs=in_specs, out_specs=out_specs, check_vma=False)
```

profile of v0, /device:TPU:0, one launch (start us, length us, event | category | flops | bytes accessed | tf_op | source)
XLA Modules:
  0.0 290.6 jit_solution(196216083540338696)
XLA Ops:
  8.2 3.0 %collective-permute-start = (bf16[128,512]{1,0:T(8,128)(2,1)S(1)}, bf16[128,512]{1,0:T(8,128)(2,1)S(1)}, u32[]{:S(2)}, u32[]{:S(2)}) collective-permute-start(bf16[128,512]{1,0:T(8,128)(2,1)S(1)} %get-tuple-element.64), channel_id=1, source_target_pairs={{0,1},{1,0},{2,3},{3,2},{4,5},{5,4},{6,7},{7,6},{8,9},{9,8},{10,11... | collective-permute-start | bytes 393224 | tf_op jit(solution)/shard_map/ppermute | solution.py:12
  12.4 2.8 collective-permute-done
  15.2 2.0 collective-permute-start.1
  17.6 1.8 collective-permute-start.7
  20.8 3.2 %collective-permute-start.2 = (bf16[128,512]{1,0:T(8,128)(2,1)S(1)}, bf16[128,512]{1,0:T(8,128)(2,1)S(1)}, u32[]{:S(2)}, u32[]{:S(2)}) collective-permute-start(bf16[128,512]{1,0:T(8,128)(2,1)S(1)} %collective-permute-done.1), channel_id=1, source_target_pairs={{0,4},{1,5},{2,6},{3,7},{4,0},{5,1},{6,2},{7,3},{8,12},{9,13},{10,... | collective-permute-start | bytes 393224 | tf_op jit(solution)/shard_map/ppermute | solution.py:12
  24.3 2.4 collective-permute-start.8
  26.8 6.2 %collective-permute-done.2 = bf16[128,512]{1,0:T(8,128)(2,1)S(1)} collective-permute-done((bf16[128,512]{1,0:T(8,128)(2,1)S(1)}, bf16[128,512]{1,0:T(8,128)(2,1)S(1)}, u32[]{:S(2)}, u32[]{:S(2)}) %collective-permute-start.2) | collective-permute-done | bytes 131104 | tf_op jit(solution)/shard_map/ppermute | solution.py:12
  37.3 5.2 %all-to-all-start.2 = ((bf16[2,512,128]{2,0,1:T(2,128)(2,1)}), bf16[2,512,128]{2,0,1:T(2,128)(2,1)S(1)}, u32[]{:S(2)}, u32[]{:S(2)}) async-start(bf16[2,512,128]{2,0,1:T(2,128)(2,1)} %copy.140), calls=%async_computation.2 | async-start | bytes 524288 | tf_op jit(solution)/shard_map/all_to_all | solution.py:97
  44.5 6.3 %all-to-all-done.2 = bf16[2,512,128]{2,0,1:T(2,128)(2,1)S(1)} async-done(((bf16[2,512,128]{2,0,1:T(2,128)(2,1)}), bf16[2,512,128]{2,0,1:T(2,128)(2,1)S(1)}, u32[]{:S(2)}, u32[]{:S(2)}) %all-to-all-start.2) | async-done | bytes 262176 | tf_op jit(solution)/shard_map/all_to_all | solution.py:97
  50.8 4.2 %all-to-all-start = ((bf16[2,512,128]{2,0,1:T(2,128)(2,1)}), bf16[2,512,128]{2,0,1:T(2,128)(2,1)}, u32[]{:S(2)}, u32[]{:S(2)}) async-start(bf16[2,512,128]{2,0,1:T(2,128)(2,1)} %copy.122), calls=%async_computation | async-start | bytes 524288 | tf_op jit(solution)/shard_map/all_to_all | solution.py:97
  56.7 1.5 convolution_bitcast_fusion
  58.9 2.0 copy.142
  60.9 3.1 %convolution_bitcast_fusion.1 = f32[2,64,64,32]{1,2,3,0:T(8,128)} fusion(bf16[2,64,32,32]{1,3,2,0:T(8,128)(2,1)} %bitcast.316, f32[1,2,64,64]{3,2,1,0:T(8,128)S(1)} %get-tuple-element.66, f32[1,2,64,64]{3,2,1,0:T(8,128)S(1)} %get-tuple-element.77), kind=kOutput, calls=%fused_computation.41 | convolution fusion | flops 100671488 | bytes 1376256 | tf_op jit(solution)/shard_map/brnm,abnk->arkm/dot_general | solution.py:50
  64.0 1.7 copy.123
  65.7 2.0 copy.124
  67.7 1.9 convolution_bitcast_fusion.2
  69.6 2.6 multiply_add_fusion.4
  72.4 2.7 copy.129
  75.2 1.7 pad_maximum_fusion.3
  76.9 2.7 copy.144
  79.6 2.8 fusion.28
  85.0 2.4 fusion.37
  87.3 3.3 %copy.146 = f32[2,32,64,64]{2,3,1,0:T(8,128)} copy(f32[2,32,64,64]{3,1,2,0:T(8,128)} %fusion.37) | data formatting | bytes 2097152 | tf_op jit(solution)/shard_map/brkj,abjm->arkm/dot_general | solution.py:64
  90.7 3.2 %pad_maximum_fusion = f32[2,64,64,32]{1,2,3,0:T(8,128)} fusion(f32[1,64,64,32]{1,2,3,0:T(8,128)} %get-tuple-element.75, f32[1,64,64,32]{1,2,3,0:T(8,128)} %get-tuple-element.76), kind=kLoop, calls=%fused_computation.1 | loop fusion | flops 262144 | bytes 2097152 | tf_op jit(solution)/shard_map/stack | solution.py:51
  93.9 3.8 %copy.126 = f32[2,64,64,32]{2,3,0,1:T(8,128)} copy(f32[2,64,64,32]{1,2,3,0:T(8,128)} %pad_maximum_fusion) | data formatting | bytes 2097152 | tf_op jit(solution)/shard_map/stack | solution.py:51
  97.7 2.8 fusion.25
  100.5 2.1 multiply_add_fusion.1
  103.7 2.2 copy.131
  105.9 2.6 fusion.40
  108.5 2.3 copy.160
  110.8 4.4 %multiply_subtract_fusion = (f32[1,64,64,32]{1,2,3,0:T(8,128)S(1)}, f32[1,64,64,32]{1,2,3,0:T(8,128)}, f32[1,64,64,32]{1,2,3,0:T(8,128)S(1)}, f32[1,64,64,32]{1,...) fusion(f32[2,64,64,32]{1,2,3,0:T(8,128)} %bitcast.299, f32[64,32]{0,1:T(8,128)S(1)} %get-tuple-element.89, ...), kind=kLoop, calls=%fused_computation.77 | loop fusion | flops 2359296 | bytes 6307840 | tf_op jit(solution)/shard_map/sub | solution.py:66
  117.5 2.1 reshape.296
  119.6 5.7 %all-to-all-start.3 = ((bf16[8,2,8192]{2,1,0:T(2,128)(2,1)}), bf16[8,2,8192]{2,1,0:T(2,128)(2,1)}, u32[]{:S(2)}, u32[]{:S(2)}) async-start(bf16[8,2,8192]{2,1,0:T(2,128)(2,1)} %reshape.296), calls=%async_computation.3 | async-start | bytes 524288 | tf_op jit(solution)/shard_map/all_to_all | solution.py:101
  125.3 1.9 fusion.52
  129.1 4.5 %all-to-all-done.3 = bf16[8,2,8192]{2,1,0:T(2,128)(2,1)} async-done(((bf16[8,2,8192]{2,1,0:T(2,128)(2,1)}), bf16[8,2,8192]{2,1,0:T(2,128)(2,1)}, u32[]{:S(2)}, u32[]{:S(2)}) %all-to-all-start.3) | async-done | bytes 262176 | tf_op jit(solution)/shard_map/all_to_all | solution.py:101
  133.7 4.1 %all-to-all-start.1 = ((bf16[8,2,8192]{2,1,0:T(2,128)(2,1)}), bf16[8,2,8192]{2,1,0:T(2,128)(2,1)}, u32[]{:S(2)}, u32[]{:S(2)}) async-start(bf16[8,2,8192]{2,1,0:T(2,128)(2,1)} %reshape.294), calls=%async_computation.1 | async-start | bytes 524288 | tf_op jit(solution)/shard_map/all_to_all | solution.py:101
  141.1 4.8 %all-to-all-done.1 = bf16[8,2,8192]{2,1,0:T(2,128)(2,1)} async-done(((bf16[8,2,8192]{2,1,0:T(2,128)(2,1)}), bf16[8,2,8192]{2,1,0:T(2,128)(2,1)}, u32[]{:S(2)}, u32[]{:S(2)}) %all-to-all-start.1) | async-done | bytes 262176 | tf_op jit(solution)/shard_map/all_to_all | solution.py:101
  152.2 2.1 maximum_multiply_fusion
  154.3 3.5 %copy.204 = f32[512,1536]{1,0:T(8,128)} copy(f32[512,1536]{0,1:T(8,128)} %maximum_multiply_fusion) | data formatting | bytes 6291456
  158.5 1.9 fusion.65
  161.9 2.1 collective-permute-start.3
  164.3 9.5 %collective-permute-done.3 = bf16[512,128]{0,1:T(8,128)(2,1)S(1)} collective-permute-done((bf16[512,128]{0,1:T(8,128)(2,1)S(1)}, bf16[512,128]{0,1:T(8,128)(2,1)S(1)}, u32[]{:S(2)}, u32[]{:S(2)}) %collective-permute-start.3) | collective-permute-done | bytes 131104 | tf_op jit(solution)/shard_map/ppermute | solution.py:12
  174.2 13.3 %collective-permute-done.4 = bf16[512,128]{0,1:T(8,128)(2,1)S(1)} collective-permute-done((bf16[512,128]{0,1:T(8,128)(2,1)S(1)}, bf16[512,128]{0,1:T(8,128)(2,1)S(1)}, u32[]{:S(2)}, u32[]{:S(2)}) %collective-permute-start.4) | collective-permute-done | bytes 131104 | tf_op jit(solution)/shard_map/ppermute | solution.py:12
  188.0 16.3 %collective-permute-done.5 = bf16[512,128]{0,1:T(8,128)(2,1)S(1)} collective-permute-done((bf16[512,128]{0,1:T(8,128)(2,1)S(1)}, bf16[512,128]{0,1:T(8,128)(2,1)S(1)}, u32[]{:S(2)}, u32[]{:S(2)}) %collective-permute-start.5) | collective-permute-done | bytes 131104 | tf_op jit(solution)/shard_map/ppermute | solution.py:12
  207.0 7.8 %collective-permute-done.11 = bf16[2,512,128]{1,2,0:T(8,128)(2,1)S(1)} collective-permute-done((bf16[2,512,128]{1,2,0:T(8,128)(2,1)S(1)}, bf16[2,512,128]{1,2,0:T(8,128)(2,1)S(1)}, u32[]{:S(2)}, u32[]{:S(2)}) %collective-permute-start.11) | collective-permute-done | bytes 262176 | tf_op jit(solution)/shard_map/ppermute | solution.py:12
  216.3 27.5 %reduce-scatter.4.cloned.1.call-done = f32[64,1536]{1,0:T(8,128)} async-done(((f32[512,1536]{1,0:T(8,128)}), f32[64,1536]{1,0:T(8,128)}) %reduce-scatter.4.cloned.1.call-update) | async-done | bytes 393232
  243.8 1.9 copy.205
  246.5 33.0 %all-reduce.4.cloned.1.call-done = (bf16[64,1536]{0,1:T(8,128)(2,1)}, bf16[64,1024]{0,1:T(8,128)(2,1)}) async-done(((bf16[64,1536]{0,1:T(8,128)(2,1)}, bf16[64,1024]{0,1:T(8,128)(2,1)}), (bf16[64,1536]{0,1:T(8,128)(2,1)}, bf16[64,1024]{0,1:T(8,128)(2,1)})) %all-reduce.4.cloned.1.call-update) | async-done | bytes 327696 | tf_op jit(solution)/shard_map/psum | solution.py:180
  (152 shorter events, 42.7 us)
Async XLA Ops:
  7.2 28.1 %copy-start = (bf16[512,512]{1,0:T(8,128)(2,1)S(1)}, bf16[512,512]{1,0:T(8,128)(2,1)}, u32[]{:S(2)}) copy-start(bf16[512,512]{1,0:T(8,128)(2,1)} %param.9) | copy-start | bytes 1572868
  8.2 131.6 %copy-start.9 = (bf16[1,128,512]{2,1,0:T(8,128)(2,1)}, bf16[1,128,512]{2,1,0:T(8,128)(2,1)S(1)}, u32[]{:S(2)}) copy-start(bf16[1,128,512]{2,1,0:T(8,128)(2,1)S(1)} %get-tuple-element.63) | copy-start | bytes 393220
  8.2 6.9 %collective-permute-start = (bf16[128,512]{1,0:T(8,128)(2,1)S(1)}, bf16[128,512]{1,0:T(8,128)(2,1)S(1)}, u32[]{:S(2)}, u32[]{:S(2)}) collective-permute-start(bf16[128,512]{1,0:T(8,128)(2,1)S(1)} %get-tuple-element.64), channel_id=1, source_target_pairs={{0,1},{1,0},{2,3},{3,2},{4,5},{5,4},{6,7},{7,6},{8,9},{9,8},{10,11... | collective-permute-start | bytes 393224 | tf_op jit(solution)/shard_map/ppermute | solution.py:12
  12.3 25.0 %copy-start.14 = (bf16[1,128,512]{2,1,0:T(8,128)(2,1)}, bf16[1,128,512]{2,1,0:T(8,128)(2,1)S(1)}, u32[]{:S(2)}) copy-start(bf16[1,128,512]{2,1,0:T(8,128)(2,1)S(1)} %get-tuple-element.61) | copy-start | bytes 393220
  12.3 5.3 %collective-permute-start.6 = (bf16[128,512]{1,0:T(8,128)(2,1)S(1)}, bf16[128,512]{1,0:T(8,128)(2,1)S(1)}, u32[]{:S(2)}, u32[]{:S(2)}) collective-permute-start(bf16[128,512]{1,0:T(8,128)(2,1)S(1)} %get-tuple-element.62), channel_id=1, source_target_pairs={{0,1},{1,0},{2,3},{3,2},{4,5},{5,4},{6,7},{7,6},{8,9},{9,8},{10,11... | collective-permute-start | bytes 393224 | tf_op jit(solution)/shard_map/ppermute | solution.py:12
  15.2 5.6 %collective-permute-start.1 = (bf16[128,512]{1,0:T(8,128)(2,1)S(1)}, bf16[128,512]{1,0:T(8,128)(2,1)S(1)}, u32[]{:S(2)}, u32[]{:S(2)}) collective-permute-start(bf16[128,512]{1,0:T(8,128)(2,1)S(1)} %collective-permute-done), channel_id=1, source_target_pairs={{0,2},{1,3},{2,0},{3,1},{4,6},{5,7},{6,4},{7,5},{8,10},{9,11},{10,... | collective-permute-start | bytes 393224 | tf_op jit(solution)/shard_map/ppermute | solution.py:12
  17.3 38.7 %copy-start.25 = (f32[1,64,64]{2,1,0:T(8,128)}, f32[1,64,64]{2,1,0:T(8,128)S(1)}, u32[]{:S(2)}) copy-start(f32[1,64,64]{2,1,0:T(8,128)S(1)} %fusion.120) | copy-start | bytes 49156
  17.6 6.8 %collective-permute-start.7 = (bf16[128,512]{1,0:T(8,128)(2,1)S(1)}, bf16[128,512]{1,0:T(8,128)(2,1)S(1)}, u32[]{:S(2)}, u32[]{:S(2)}) collective-permute-start(bf16[128,512]{1,0:T(8,128)(2,1)S(1)} %collective-permute-done.6), channel_id=1, source_target_pairs={{0,2},{1,3},{2,0},{3,1},{4,6},{5,7},{6,4},{7,5},{8,10},{9,11},{10,... | collective-permute-start | bytes 393224 | tf_op jit(solution)/shard_map/ppermute | solution.py:12
  20.8 12.2 %collective-permute-start.2 = (bf16[128,512]{1,0:T(8,128)(2,1)S(1)}, bf16[128,512]{1,0:T(8,128)(2,1)S(1)}, u32[]{:S(2)}, u32[]{:S(2)}) collective-permute-start(bf16[128,512]{1,0:T(8,128)(2,1)S(1)} %collective-permute-done.1), channel_id=1, source_target_pairs={{0,4},{1,5},{2,6},{3,7},{4,0},{5,1},{6,2},{7,3},{8,12},{9,13},{10,... | collective-permute-start | bytes 393224 | tf_op jit(solution)/shard_map/ppermute | solution.py:12
  24.2 31.8 %copy-start.27 = (f32[1,64,64]{2,1,0:T(8,128)}, f32[1,64,64]{2,1,0:T(8,128)S(1)}, u32[]{:S(2)}) copy-start(f32[1,64,64]{2,1,0:T(8,128)S(1)} %get-tuple-element.87) | copy-start | bytes 49156
  24.3 10.5 %collective-permute-start.8 = (bf16[128,512]{1,0:T(8,128)(2,1)S(1)}, bf16[128,512]{1,0:T(8,128)(2,1)S(1)}, u32[]{:S(2)}, u32[]{:S(2)}) collective-permute-start(bf16[128,512]{1,0:T(8,128)(2,1)S(1)} %collective-permute-done.7), channel_id=1, source_target_pairs={{0,4},{1,5},{2,6},{3,7},{4,0},{5,1},{6,2},{7,3},{8,12},{9,13},{10,... | collective-permute-start | bytes 393224 | tf_op jit(solution)/shard_map/ppermute | solution.py:12
  34.8 8.5 %copy-start.11 = (bf16[512,512]{1,0:T(8,128)(2,1)S(1)}, bf16[512,512]{1,0:T(8,128)(2,1)}, u32[]{:S(2)}) copy-start(bf16[512,512]{1,0:T(8,128)(2,1)} %param.8) | copy-start | bytes 1572868
  35.3 8.3 %copy-start.13 = (bf16[128,512]{1,0:T(8,128)(2,1)}, bf16[128,512]{1,0:T(8,128)(2,1)S(1)}, u32[]{:S(2)}) copy-start(bf16[128,512]{1,0:T(8,128)(2,1)S(1)} %rev.24) | copy-start | bytes 393220
  36.4 19.3 %copy-start.29 = (f32[64,1024]{1,0:T(8,128)S(1)}, f32[64,1024]{1,0:T(8,128)}, u32[]{:S(2)}) copy-start(f32[64,1024]{1,0:T(8,128)} %param.10) | copy-start | bytes 786436
  37.3 13.5 %all-to-all-start.2 = ((bf16[2,512,128]{2,0,1:T(2,128)(2,1)}), bf16[2,512,128]{2,0,1:T(2,128)(2,1)S(1)}, u32[]{:S(2)}, u32[]{:S(2)}) async-start(bf16[2,512,128]{2,0,1:T(2,128)(2,1)} %copy.140), calls=%async_computation.2 | async-start | bytes 524288 | tf_op jit(solution)/shard_map/all_to_all | solution.py:97
  50.8 5.9 %copy-start.17 = (bf16[2,512,128]{2,0,1:T(2,128)(2,1)}, bf16[2,512,128]{2,0,1:T(2,128)(2,1)S(1)}, u32[]{:S(2)}) copy-start(bf16[2,512,128]{2,0,1:T(2,128)(2,1)S(1)} %all-to-all-done.2) | copy-start | bytes 786436
  50.8 13.2 %all-to-all-start = ((bf16[2,512,128]{2,0,1:T(2,128)(2,1)}), bf16[2,512,128]{2,0,1:T(2,128)(2,1)}, u32[]{:S(2)}, u32[]{:S(2)}) async-start(bf16[2,512,128]{2,0,1:T(2,128)(2,1)} %copy.122), calls=%async_computation | async-start | bytes 524288 | tf_op jit(solution)/shard_map/all_to_all | solution.py:97
  56.7 1.5 copy-start.18
  67.7 2.0 copy-start.4
  67.7 2.0 copy-start.31
  76.9 2.8 copy-start.23
  76.9 2.8 copy-start.24
  79.6 2.8 copy-start.3
  83.5 1.4 copy-start.1
  83.6 1.4 copy-start.21
  83.6 1.4 copy-start.22
  97.7 2.8 copy-start.2
  110.8 4.4 %copy-start.19 = (f32[1,2,64,64]{3,2,1,0:T(8,128)S(1)}, f32[1,2,64,64]{3,2,1,0:T(8,128)}, u32[]{:S(2)}) copy-start(f32[1,2,64,64]{3,2,1,0:T(8,128)} %get-tuple-element.65) | copy-start | bytes 98308
  110.8 4.4 %copy-start.20 = (f32[1,2,64,64]{3,2,1,0:T(8,128)S(1)}, f32[1,2,64,64]{3,2,1,0:T(8,128)}, u32[]{:S(2)}) copy-start(f32[1,2,64,64]{3,2,1,0:T(8,128)} %get-tuple-element.78) | copy-start | bytes 98308
  119.6 14.1 %all-to-all-start.3 = ((bf16[8,2,8192]{2,1,0:T(2,128)(2,1)}), bf16[8,2,8192]{2,1,0:T(2,128)(2,1)}, u32[]{:S(2)}, u32[]{:S(2)}) async-start(bf16[8,2,8192]{2,1,0:T(2,128)(2,1)} %reshape.296), calls=%async_computation.3 | async-start | bytes 524288 | tf_op jit(solution)/shard_map/all_to_all | solution.py:101
  133.7 12.3 %all-to-all-start.1 = ((bf16[8,2,8192]{2,1,0:T(2,128)(2,1)}), bf16[8,2,8192]{2,1,0:T(2,128)(2,1)}, u32[]{:S(2)}, u32[]{:S(2)}) async-start(bf16[8,2,8192]{2,1,0:T(2,128)(2,1)} %reshape.294), calls=%async_computation.1 | async-start | bytes 524288 | tf_op jit(solution)/shard_map/all_to_all | solution.py:101
  137.7 106.0 %reduce-scatter.4.cloned.1.call-start = ((), (), s32[]{:S(2)}) async-start(), calls=%async_computation.5 | async-start | bytes 3538944
  148.9 2.9 copy-start.10
  150.4 1.4 copy-start.7
  150.4 1.8 copy-start.6
  157.8 3.7 %copy-start.8 = (bf16[2,512,128]{1,2,0:T(8,128)(2,1)S(1)}, bf16[2,512,128]{1,2,0:T(8,128)(2,1)}, u32[]{:S(2)}) copy-start(bf16[2,512,128]{1,2,0:T(8,128)(2,1)} %copy-done.7) | copy-start | bytes 786436
  157.8 121.7 %all-reduce.4.cloned.1.call-start = ((), (), s32[]{:S(2)}) async-start(), calls=%async_computation.6 | async-start | bytes 1310720 | tf_op jit(solution)/shard_map/psum | solution.py:180
  160.4 3.5 %copy-start.5 = (bf16[512,512]{1,0:T(8,128)(2,1)S(1)}, bf16[512,512]{1,0:T(8,128)(2,1)}, u32[]{:S(2)}) copy-start(bf16[512,512]{1,0:T(8,128)(2,1)} %param.7) | copy-start | bytes 1572868
  161.3 12.6 %copy-start.12 = (bf16[512,512]{1,0:T(8,128)(2,1)S(1)}, bf16[512,512]{1,0:T(8,128)(2,1)}, u32[]{:S(2)}) copy-start(bf16[512,512]{1,0:T(8,128)(2,1)} %param.8) | copy-start | bytes 1572868
  161.3 12.6 %copy-start.16 = (bf16[1,128,1024]{2,1,0:T(8,128)(2,1)S(1)}, bf16[1,128,1024]{2,1,0:T(8,128)(2,1)}, u32[]{:S(2)}) copy-start(bf16[1,128,1024]{2,1,0:T(8,128)(2,1)} %param.11) | copy-start | bytes 786436
  161.6 26.2 %copy-start.15 = (bf16[1,128,1024]{2,1,0:T(8,128)(2,1)S(1)}, bf16[1,128,1024]{2,1,0:T(8,128)(2,1)}, u32[]{:S(2)}) copy-start(bf16[1,128,1024]{2,1,0:T(8,128)(2,1)} %param.6) | copy-start | bytes 786436
  161.8 25.7 %collective-permute-start.9 = (bf16[2,512,128]{1,2,0:T(8,128)(2,1)S(1)}, bf16[2,512,128]{1,2,0:T(8,128)(2,1)}, u32[]{:S(2)}, u32[]{:S(2)}) collective-permute-start(bf16[2,512,128]{1,2,0:T(8,128)(2,1)S(1)} %pad_maximum_fusion.9), channel_id=1, source_target_pairs={{0,1},{1,0},{2,3},{3,2},{4,5},{5,4},{6,7},{7,6},{8,9},{9,8},{10,11... | collective-permute-start | bytes 786440 | tf_op jit(solution)/shard_map/ppermute | solution.py:12
  161.9 11.9 %collective-permute-start.3 = (bf16[512,128]{0,1:T(8,128)(2,1)S(1)}, bf16[512,128]{0,1:T(8,128)(2,1)S(1)}, u32[]{:S(2)}, u32[]{:S(2)}) collective-permute-start(bf16[512,128]{0,1:T(8,128)(2,1)S(1)} %slice_bitcast_fusion.2), channel_id=1, source_target_pairs={{0,1},{1,0},{2,3},{3,2},{4,5},{5,4},{6,7},{7,6},{8,9},{9,8},{10,11... | collective-permute-start | bytes 393224 | tf_op jit(solution)/shard_map/ppermute | solution.py:12
  173.8 13.7 %collective-permute-start.4 = (bf16[512,128]{0,1:T(8,128)(2,1)S(1)}, bf16[512,128]{0,1:T(8,128)(2,1)S(1)}, u32[]{:S(2)}, u32[]{:S(2)}) collective-permute-start(bf16[512,128]{0,1:T(8,128)(2,1)S(1)} %collective-permute-done.3), channel_id=1, source_target_pairs={{0,2},{1,3},{2,0},{3,1},{4,6},{5,7},{6,4},{7,5},{8,10},{9,11},{10,... | collective-permute-start | bytes 393224 | tf_op jit(solution)/shard_map/ppermute | solution.py:12
  187.5 16.7 %collective-permute-start.5 = (bf16[512,128]{0,1:T(8,128)(2,1)S(1)}, bf16[512,128]{0,1:T(8,128)(2,1)S(1)}, u32[]{:S(2)}, u32[]{:S(2)}) collective-permute-start(bf16[512,128]{0,1:T(8,128)(2,1)S(1)} %collective-permute-done.4), channel_id=1, source_target_pairs={{0,4},{1,5},{2,6},{3,7},{4,0},{5,1},{6,2},{7,3},{8,12},{9,13},{10,... | collective-permute-start | bytes 393224 | tf_op jit(solution)/shard_map/ppermute | solution.py:12
  187.5 17.5 %collective-permute-start.10 = (bf16[2,512,128]{1,2,0:T(8,128)(2,1)}, bf16[2,512,128]{1,2,0:T(8,128)(2,1)S(1)}, u32[]{:S(2)}, u32[]{:S(2)}) collective-permute-start(bf16[2,512,128]{1,2,0:T(8,128)(2,1)} %collective-permute-done.9), channel_id=1, source_target_pairs={{0,2},{1,3},{2,0},{3,1},{4,6},{5,7},{6,4},{7,5},{8,10},{9,11},{10,... | collective-permute-start | bytes 786440 | tf_op jit(solution)/shard_map/ppermute | solution.py:12
  205.0 9.8 %collective-permute-start.11 = (bf16[2,512,128]{1,2,0:T(8,128)(2,1)S(1)}, bf16[2,512,128]{1,2,0:T(8,128)(2,1)S(1)}, u32[]{:S(2)}, u32[]{:S(2)}) collective-permute-start(bf16[2,512,128]{1,2,0:T(8,128)(2,1)S(1)} %collective-permute-done.10), channel_id=1, source_target_pairs={{0,4},{1,5},{2,6},{3,7},{4,0},{5,1},{6,2},{7,3},{8,12},{9,13},{10,... | collective-permute-start | bytes 786440 | tf_op jit(solution)/shard_map/ppermute | solution.py:12
  279.5 3.5 %copy-start.30 = (bf16[64,1024]{0,1:T(8,128)(2,1)S(1)}, bf16[64,1024]{0,1:T(8,128)(2,1)}, u32[]{:S(2)}) copy-start(bf16[64,1024]{0,1:T(8,128)(2,1)} %get-tuple-element.31) | copy-start | bytes 393220
  (2 other events, 1.5 us)
Sparse Core Ops, SparseCore 0:
  157.9 85.8 reduce-scatter.3
  246.3 33.2 all-reduce.3
where the time goes:
time: 292 us; the launch traced here: 291 us
  waiting for transfers between devices  134 us (46%)
  local copies, waits for them, and re-layouts  52.8 us (18%)
  starting transfers between devices  35.6 us (12%)
  matrix products  31.2 us (11%)
  other arithmetic  22.3 us (8%)
  between operations  14.8 us (5%)
    ppermute x12, waiting for transfers between devices, swapped(): lax.ppermute(x, axis, [(i, i ^ 1 << stride) for i in range(lax.axis_size(...  57.8 us
    psum x1, waiting for transfers between devices, body(): lax.psum(share.astype(jnp.bfloat16), 'batch').astype(jnp.float32)  33 us
    unnamed x3, waiting for transfers between devices  27.5 us
    unnamed x76, local copies, waits for them, and re-layouts  16.4 us
    ppermute x12, starting transfers between devices, swapped(): lax.ppermute(x, axis, [(i, i ^ 1 << stride) for i in range(lax.axis_size(...  16.2 us
    all_to_all x2, starting transfers between devices, to_tokens(): lax.all_to_all(stacked, 'seq', split_axis=2, concat_axis=1, tiled=True)  9.78 us
    all_to_all x2, starting transfers between devices, to_channels(): lax.all_to_all(stacked, 'seq', split_axis=1, concat_axis=2, tiled=True)  9.47 us
    all_to_all x2, waiting for transfers between devices, to_tokens(): lax.all_to_all(stacked, 'seq', split_axis=2, concat_axis=1, tiled=True)  9.38 us
  transfers between devices with their start and end apart: 18, of which 14 were waited for; matrix products, arithmetic and copies ran while one was open for 10% of the time, Pallas kernels for 0%

commit v1 on v0

--- a/solution.py
+++ b/solution.py
@@ -1,8 +1,12 @@
+import functools
 import math
 
 import jax
 import jax.numpy as jnp
+import numpy as np
 from jax import lax
+from jax.experimental import pallas as pl
+from jax.experimental.pallas import tpu as pltpu
 from jax.sharding import PartitionSpec as P
 
 precise = lax.Precision.HIGH
@@ -189,6 +193,259 @@
         filter_total,
     )
 
+MESH = pl.DeviceIdType.MESH
+
+
+def angle_parts(length):
+    step = 1 << (length.bit_length() - 1) // 2
+    angle = np.pi * (np.arange(length) + 0.5)[None] / length
+    coarse = np.arange(length // step)[:, None] * step * angle
+    fine = np.arange(step)[:, None] * angle
+    return (
+        np.stack([np.cos(coarse), np.sin(coarse)]).astype(np.float32),
+        np.stack([np.cos(fine), np.sin(fine)]).astype(np.float32),
+    )
+
+
+def matmul(left, right):
+    return jnp.dot(left, right, preferred_element_type=jnp.float32)
+
+
+def matmul_t(left, right):
+    return lax.dot_general(
+        left, right, (((1,), (1,)), ((), ())), preferred_element_type=jnp.float32
+    )
+
+
+def times(x, h, conj):
+    size = x.shape[1] // 2
+    xr, xs, hr, hs = x[:, :size], x[:, size:], h[:, :size], h[:, size:]
+    if conj:
+        return xr * hr + xs * hs, xs * hr - xr * hs
+    return xr * hr - xs * hs, xr * hs + xs * hr
+
+
+def fused(
+    peers, scale,
+    tok, wq, wv, wo, taps, cot, coarse, fine,
+    block, grad_tok, grad_w, grad_f,
+    table, strands, ups, strands_t, query, gates, send1, recv1, send2, recv2,
+    vspec, gspec, hspec, yspec,
+    ssem1, rsem1, lsem1, ssem2, rsem2, lsem2,
+):
+    f32, b16 = jnp.float32, jnp.bfloat16
+    me = lax.axis_index("seq")
+    here, half = tok.shape[0], wq.shape[0]
+    own = half // peers
+    length = here * peers
+
+    barrier = pltpu.get_barrier_semaphore()
+    for r in range(1, peers):
+        pl.semaphore_signal(
+            barrier, inc=1, device_id={"seq": lax.rem(me + r, peers)}, device_id_type=MESH
+        )
+    flip = (
+        lax.broadcasted_iota(jnp.int32, (half, half), 0)
+        + lax.broadcasted_iota(jnp.int32, (half, half), 1)
+        == half - 1
+    ).astype(f32).astype(b16)
+    strands[:here] = tok[:, :half]
+    strands[here:] = matmul(tok[:, half:], flip).astype(b16)
+    value = matmul(strands[...], wv[...]).astype(b16)
+    send1[0] = value[:here].T
+    send1[1] = value[here:].T
+    pl.semaphore_wait(barrier, peers - 1)
+
+    def rows_of(p):
+        return pl.ds(pl.multiple_of(p * own, own), own)
+
+    def lanes_of(p):
+        return pl.ds(pl.multiple_of(p * here, here), here)
+
+    def out1(part):
+        pair = pl.ds(2 * part, 2)
+        copies = []
+        for r in range(1, peers):
+            p = lax.rem(me + r, peers)
+            copies.append(
+                pltpu.make_async_remote_copy(
+                    src_ref=send1.at[pair, rows_of(p), :],
+                    dst_ref=recv1.at[pair, :, lanes_of(me)],
+                    send_sem=ssem1.at[part, r],
+                    recv_sem=rsem1.at[part, r],
+                    device_id={"seq": p},
+                    device_id_type=MESH,
+                )
+            )
+        copies.append(
+            pltpu.make_async_copy(
+                send1.at[pair, rows_of(me), :], recv1.at[pair, :, lanes_of(me)], lsem1.at[part]
+            )
+        )
+        for c in copies:
+            c.start()
+        return copies
+
+    def out2(part):
+        pair = pl.ds(2 * part, 2)
+        copies = []
+        for r in range(1, peers):
+            p = lax.rem(me + r, peers)
+            copies.append(
+                pltpu.make_async_remote_copy(
+                    src_ref=send2.at[pair, :, lanes_of(p)],
+                    dst_ref=recv2.at[pair, rows_of(me), :],
+                    send_sem=ssem2.at[part, r],
+                    recv_sem=rsem2.at[part, r],
+                    device_id={"seq": p},
+                    device_id_type=MESH,
+                )
+            )
+        copies.append(
+            pltpu.make_async_copy(
+                send2.at[pair, :, lanes_of(me)], recv2.at[pair, rows_of(me), :], lsem2.at[part]
+            )
+        )
+        for c in copies:
+            c.start()
+        return copies
+
+    first = out1(0)
+    ups[:here] = cot[:, :half]
+    ups[here:] = matmul(cot[:, half:], flip).astype(b16)
+    query[...] = matmul(strands[...], wq[...]).astype(b16)
+    gates[...] = matmul_t(ups[...], wo[...]).astype(b16)
+    grad_conv = (gates[...].astype(f32) * query[...].astype(f32)).astype(b16)
+    send1[2] = grad_conv[:here].T
+    send1[3] = grad_conv[here:].T
+    second = out1(1)
+
+    count, step = coarse.shape[1], fine.shape[1]
+
+    @pl.loop(0, count)
+    def _(a):
+        ca, sa = coarse[0, pl.ds(a, 1), :], coarse[1, pl.ds(a, 1), :]
+        rows = pl.ds(pl.multiple_of(a * step, step), step)
+        table[rows, :length] = (ca * fine[0] - sa * fine[1]).astype(b16)
+        table[rows, length:] = (sa * fine[0] + ca * fine[1]).astype(b16)
+
+    strands_t[...] = strands[...].T
+    hspec[...] = matmul(taps[...].astype(b16), table[...])
+
+    def spread(part, causal):
+        spec = (vspec, gspec)[part]
+        for strand in range(2):
+            row = pl.ds(strand * own, own)
+            r, s = times(spec[row, :], hspec[...], strand != causal)
+            yspec[row, :length] = r.astype(b16)
+            yspec[row, length:] = s.astype(b16)
+        back = (matmul_t(yspec[...], table[...]) * (1.0 / length)).astype(b16)
+        send2[2 * part] = back[:own]
+        send2[2 * part + 1] = back[own:]
+
+    for c in first:
+        c.wait()
+    vspec[...] = matmul(recv1[0:2].reshape(2 * own, length), table[...])
+    spread(0, 0)
+    third = out2(0)
+    for c in second:
+        c.wait()
+    gspec[...] = matmul(recv1[2:4].reshape(2 * own, length), table[...])
+    spread(1, 1)
+    fourth = out2(1)
+    r0, s0 = times(gspec[:own, :], vspec[:own, :], True)
+    r1, s1 = times(vspec[own:, :], gspec[own:, :], True)
+    yspec[:own, :length] = (r0 + r1).astype(b16)
+    yspec[:own, length:] = (s0 + s1).astype(b16)
+    grad_f[...] = matmul_t(yspec[:own, :], table[...]) * (scale / length)
+
+    for c in third:
+        c.wait()
+    conv = jnp.concatenate([recv2[0].T, recv2[1].T], axis=0).astype(f32)
+    gated = (query[...].astype(f32) * conv).astype(b16)
+    grad_query = (gates[...].astype(f32) * conv).astype(b16)
+    grad_w[:, :half] = (matmul(strands_t[...], grad_query) * scale).astype(grad_w.dtype)
+    grad_w[:, 2 * half :] = (matmul(gated.T, ups[...]) * scale).astype(grad_w.dtype)
+    total = strands[...].astype(f32) + matmul(gated, wo[...])
+    block[:, :half] = total[:here].astype(b16)
+    block[:, half:] = matmul(total[here:].astype(b16), flip).astype(b16)
+    total = ups[...].astype(f32) + matmul_t(grad_query, wq[...])
+    for c in fourth:
+        c.wait()
+    grad_value = jnp.concatenate([recv2[2].T, recv2[3].T], axis=0)
+    grad_w[:, half : 2 * half] = (matmul(strands_t[...], grad_value) * scale).astype(grad_w.dtype)
+    total = total + matmul_t(grad_value, wv[...])
+    grad_tok[:, :half] = total[:here].astype(b16)
+    grad_tok[:, half:] = matmul(total[here:].astype(b16), flip).astype(b16)
+
+
+def short_body(tokens, w_query, w_value, w_out, long_filter, cotangent):
+    f32, b16 = jnp.float32, jnp.bfloat16
+    half = w_query.shape[0]
+    peers = lax.axis_size("seq")
+    here = tokens.shape[1]
+    length = here * peers
+    own = half // peers
+    scale = (2.0 * lax.axis_size("batch") * length) ** (-0.5)
+    coarse, fine = angle_parts(length)
+    dma = pltpu.SemaphoreType.DMA
+    block, grad_tok, grad_w, grad_f = pl.pallas_call(
+        functools.partial(fused, peers, scale),
+        out_shape=(
+            jax.ShapeDtypeStruct((here, 2 * half), b16),
+            jax.ShapeDtypeStruct((here, 2 * half), b16),
+            jax.ShapeDtypeStruct((half, 3 * half), b16),
+            jax.ShapeDtypeStruct((own, length), f32),
+        ),
+        in_specs=[pl.BlockSpec(memory_space=pltpu.VMEM)] * 8,
+        out_specs=(pl.BlockSpec(memory_space=pltpu.VMEM),) * 4,
+        scratch_shapes=[
+            pltpu.VMEM((length, 2 * length), b16),
+            pltpu.VMEM((2 * here, half), b16),
+            pltpu.VMEM((2 * here, half), b16),
+            pltpu.VMEM((half, 2 * here), b16),
+            pltpu.VMEM((2 * here, half), b16),
+            pltpu.VMEM((2 * here, half), b16),
+            pltpu.VMEM((4, half, here), b16),
+            pltpu.VMEM((4, own, length), b16),
+            pltpu.VMEM((4, own, length), b16),
+            pltpu.VMEM((4, half, here), b16),
+            pltpu.VMEM((2 * own, 2 * length), f32),
+            pltpu.VMEM((2 * own, 2 * length), f32),
+            pltpu.VMEM((own, 2 * length), f32),
+            pltpu.VMEM((2 * own, 2 * length), b16),
+            dma((2, peers)),
+            dma((2, peers)),
+            dma((2,)),
+            dma((2, peers)),
+            dma((2, peers)),
+            dma((2,)),
+        ],
+        compiler_params=pltpu.CompilerParams(
+            collective_id=0, has_side_effects=True, vmem_limit_bytes=60 << 20
+        ),
+    )(tokens[0], w_query, w_value, w_out, long_filter, cotangent[0], coarse, fine)
+    share = lax.psum_scatter(grad_w, "seq", scatter_dimension=0, tiled=True)
+    share = lax.psum(share, "batch").astype(f32)
+    total_f = lax.psum(grad_f.astype(b16), "batch").astype(f32)
+    return (
+        block[None],
+        grad_tok[None],
+        share[:, :half],
+        share[:, half : 2 * half],
+        share[:, 2 * half :],
+        total_f,
+    )
+
+
+def fits(tokens, peers):
+    return (tokens.shape[1] * peers) ** 2 * 4 <= 8 << 20
+
+
+def choose(tokens, *rest):
+    short = fits(tokens, lax.axis_size("seq"))
+    return (short_body if short else body)(tokens, *rest)
+
 
 def solution(mesh):
     in_specs = (P("batch", "seq", None), P(), P(), P(), P("seq", None), P("batch", "seq", None))
@@ -200,4 +457,4 @@
         P("seq", None),
         P("seq", None),
     )
-    return jax.shard_map(body, mesh=mesh, in_specs=in_specs, out_specs=out_specs, check_vma=False)
+    return jax.shard_map(choose, mesh=mesh, in_specs=in_specs, out_specs=out_specs, check_vma=False)

time: 292 us -> 153 us (0.52)
  local copies, waits for them, and re-layouts: 52.8 us -> 3.92 us
  starting transfers between devices: 35.6 us -> 0.08 us
  waiting for transfers between devices: 134 us -> 98.7 us
  Pallas kernels: 0 us -> 33.8 us
  matrix products: 31.2 us -> 0 us
  other arithmetic: 22.3 us -> 2.29 us
    reduce_scatter x0 -> x1, waiting for transfers between devices: none -> 64.2 us  [short_body(): share = lax.psum_scatter(grad_w, 'seq', scatter_dimension=0, tiled=True)]
    ppermute x12 -> x0, waiting for transfers between devices: 57.8 us -> none  [swapped(): lax.ppermute(x, axis, [(i, i ^ 1 << stride) for i in range(lax.axis_size(...]
    pallas_call x0 -> x1, Pallas kernels: none -> 33.8 us  [short_body(): pl.pallas_call(functools.partial(fused, peers, scale), out_shape=(jax.Sha...]
    dot_general x24 -> x0, matrix products: 31.2 us -> none  [the longest x3 6.65 us: forward_spectrum(): jnp.einsum('brkm,abmj->arkj', turned, forward_second, precision=precise)]
    unnamed x3 -> x2, waiting for transfers between devices: 27.5 us -> 0.03 us
    all_to_all x4 -> x0, starting transfers between devices: 19.3 us -> none  [the longest x2 9.78 us: to_tokens(): lax.all_to_all(stacked, 'seq', split_axis=2, concat_axis=1, tiled=True)]
    ppermute x12 -> x0, starting transfers between devices: 16.2 us -> none  [swapped(): lax.ppermute(x, axis, [(i, i ^ 1 << stride) for i in range(lax.axis_size(...]
    all_to_all x4 -> x0, waiting for transfers between devices: 15.7 us -> none  [the longest x2 9.38 us: to_tokens(): lax.all_to_all(stacked, 'seq', split_axis=2, concat_axis=1, tiled=True)]
  transfers between devices with their start and end apart: 18 -> 2, of which waited for: 14 -> 2; matrix products, arithmetic and copies ran while one was open for 10% -> 0% of each run, Pallas kernels for 0% -> 0%
where the time goes in v1:
time: 153 us
  waiting for transfers between devices  98.7 us (65%)
  Pallas kernels  33.8 us (22%)
  between operations  14.1 us (9%)
  local copies, waits for them, and re-layouts  3.92 us (3%)
  other arithmetic  2.29 us (1%)
    reduce_scatter x1, waiting for transfers between devices, short_body(): share = lax.psum_scatter(grad_w, 'seq', scatter_dimension=0, tiled=True)  64.2 us
    psum x1, waiting for transfers between devices, short_body(): share = lax.psum(share, 'batch').astype(f32)  34.4 us
    pallas_call x1, Pallas kernels, short_body(): pl.pallas_call(functools.partial(fused, peers, scale), out_shape=(jax.Sha...  33.8 us
  transfers between devices with their start and end apart: 2, of which 2 were waited for; matrix products, arithmetic and copies ran while one was open for 0% of the time, Pallas kernels for 0%

profile of v1, /device:TPU:0, one launch (start us, length us, event | category | flops | bytes accessed | tf_op | source)
XLA Modules:
  0.0 152.9 jit_solution(6501392524716023771)
XLA Ops:
  7.2 0.0 reduce-scatter.2.cloned.1.call-start
  7.2 33.8 %shard_map.127 = (bf16[128,1024]{1,0:T(8,128)(2,1)}, bf16[128,1024]{1,0:T(8,128)(2,1)}, bf16[512,1536]{1,0:T(8,128)(2,1)}, f32[64,1024]{1,0:T(8,128)}) custom-call(bf16[128,1024]{1,0:T(8,128)(2,1)} %bitcast.6, bf16[512,512]{1,0:T(8,128)(2,1)} %wq.1, bf16[512,512]{1,0:T(8,128)(2,1)} %wv.1, bf16[512,512]{1,0:T(8,128)(2,1)} %wo.1, f32[64,1024]{1,0:T(8,128)} %taps.1, ...), custom_call_target="tpu_custom_call" | custom-call | tf_op jit(solution)/shard_map/pallas_call | solution.py:392
  41.0 0.0 copy-start
  41.0 0.0 copy-start.2
  41.0 0.0 reduce-scatter.2.cloned.1.call-update
  41.1 0.0 copy-start.1
  41.1 0.0 all-reduce.3.cloned.1.call-start
  41.1 0.8 copy-done
  42.0 0.7 convert_element_type.10
  42.6 64.2 %reduce-scatter.2.cloned.1.call-done = bf16[64,1536]{1,0:T(8,128)(2,1)} async-done(((bf16[512,1536]{1,0:T(8,128)(2,1)}), bf16[64,1536]{1,0:T(8,128)(2,1)}) %reduce-scatter.2.cloned.1.call-update) | async-done | bytes 196624 | tf_op jit(solution)/shard_map/reduce_scatter | solution.py:428
  106.9 0.0 all-reduce.3.cloned.1.call-update
  106.9 34.4 %all-reduce.3.cloned.1.call-done = (bf16[64,1536]{1,0:T(8,128)(2,1)}, bf16[64,1024]{1,0:T(8,128)(2,1)}) async-done(((bf16[64,1536]{1,0:T(8,128)(2,1)}, bf16[64,1024]{1,0:T(8,128)(2,1)}), (bf16[64,1536]{1,0:T(8,128)(2,1)}, bf16[64,1024]{1,0:T(8,128)(2,1)})) %all-reduce.3.cloned.1.call-update) | async-done | bytes 327696 | tf_op jit(solution)/shard_map/psum | solution.py:429
  141.4 1.7 %fusion = (f32[64,512]{1,0:T(8,128)}, f32[64,512]{1,0:T(8,128)}, f32[64,512]{1,0:T(8,128)}) fusion(bf16[64,1536]{1,0:T(8,128)(2,1)} %get-tuple-element.14), kind=kLoop, calls=%fused_computation | loop fusion | bytes 786432 | tf_op jit(solution)/shard_map/slice | solution.py:436
  143.0 1.6 %convert_element_type.11 = f32[64,1024]{1,0:T(8,128)} convert(bf16[64,1024]{1,0:T(8,128)(2,1)} %get-tuple-element.15) | non-fusion elementwise | flops 65536 | bytes 393216 | tf_op jit(solution)/shard_map/convert_element_type | solution.py:430
  144.6 0.0 copy-done.2
  144.6 0.7 copy.18
  145.3 0.0 copy-done.1
  145.3 0.7 copy.19
Async XLA Ops:
  7.2 99.7 %reduce-scatter.2.cloned.1.call-start = ((), (), s32[]{:S(2)}) async-start(), calls=%async_computation.1 | async-start | bytes 1769472 | tf_op jit(solution)/shard_map/reduce_scatter | solution.py:428
  41.0 1.0 copy-start
  41.0 103.6 %copy-start.2 = (bf16[128,1024]{1,0:T(8,128)(2,1)S(1)}, bf16[128,1024]{1,0:T(8,128)(2,1)}, u32[]{:S(2)}) copy-start(bf16[128,1024]{1,0:T(8,128)(2,1)} %get-tuple-element.10) | copy-start | bytes 786436
  41.1 104.3 %copy-start.1 = (bf16[128,1024]{1,0:T(8,128)(2,1)S(1)}, bf16[128,1024]{1,0:T(8,128)(2,1)}, u32[]{:S(2)}) copy-start(bf16[128,1024]{1,0:T(8,128)(2,1)} %get-tuple-element.11) | copy-start | bytes 786436
  41.1 100.3 %all-reduce.3.cloned.1.call-start = ((), (), s32[]{:S(2)}) async-start(), calls=%async_computation.2 | async-start | bytes 655360 | tf_op jit(solution)/shard_map/psum | solution.py:429
Sparse Core Ops, SparseCore 0:
  41.2 65.6 reduce-scatter.1
  109.9 31.3 all-reduce.2

commit v2 on v1

--- a/solution.py
+++ b/solution.py
@@ -228,10 +228,13 @@
 def fused(
     peers, scale,
     tok, wq, wv, wo, taps, cot, coarse, fine,
-    block, grad_tok, grad_w, grad_f,
+    block, grad_tok, out_q, out_v, out_o, out_f,
     table, strands, ups, strands_t, query, gates, send1, recv1, send2, recv2,
     vspec, gspec, hspec, yspec,
     ssem1, rsem1, lsem1, ssem2, rsem2, lsem2,
+    acc, kept, send_a, recv_a, send_b, recv_b, send_c, recv_c, full,
+    acc_f, kept_f, send_af, recv_af, send_bf, recv_bf, full_f,
+    ssem_a, rsem_a, ssem_b, rsem_b, ssem_c, rsem_c, ssem_d, rsem_d,
 ):
     f32, b16 = jnp.float32, jnp.bfloat16
     me = lax.axis_index("seq")
@@ -244,6 +247,15 @@
         pl.semaphore_signal(
             barrier, inc=1, device_id={"seq": lax.rem(me + r, peers)}, device_id_type=MESH
         )
+    batches = lax.axis_size("batch")
+    seat = lax.axis_index("batch")
+    for r in range(1, batches):
+        pl.semaphore_signal(
+            barrier, inc=1, device_id={"batch": lax.rem(seat + r, batches)}, device_id_type=MESH
+        )
+    low, high = lax.rem(seat, 2), seat // 2
+    quarter = own // batches
+    slot = 2 * low + high
     flip = (
         lax.broadcasted_iota(jnp.int32, (half, half), 0)
         + lax.broadcasted_iota(jnp.int32, (half, half), 1)
@@ -254,7 +266,7 @@
     value = matmul(strands[...], wv[...]).astype(b16)
     send1[0] = value[:here].T
     send1[1] = value[here:].T
-    pl.semaphore_wait(barrier, peers - 1)
+    pl.semaphore_wait(barrier, peers + batches - 2)
 
     def rows_of(p):
         return pl.ds(pl.multiple_of(p * own, own), own)
@@ -310,6 +322,89 @@
             c.start()
         return copies
 
+    def part_of(bit, size):
+        return pl.ds(pl.multiple_of(bit * size, size), size)
+
+    def bundle(m):
+        if m == 3:
+            return acc_f, kept_f, send_af, recv_af, send_bf, recv_bf, full_f
+        return (
+            acc.at[m], kept.at[m], send_a.at[m], recv_a.at[m], send_b.at[m], recv_b.at[m], full.at[m]
+        )
+
+    def swap(src, dst, ssem, rsem, target):
+        copy = pltpu.make_async_remote_copy(
+            src_ref=src,
+            dst_ref=dst,
+            send_sem=ssem,
+            recv_sem=rsem,
+            device_id={"batch": target},
+            device_id_type=MESH,
+        )
+        copy.start()
+        return copy
+
+    def stage_a(m):
+        total, _, out, into, _, _, _ = bundle(m)
+        out[...] = total[:, part_of(1 - low, 2 * quarter), :].astype(b16)
+        return swap(out, into, ssem_a.at[m], rsem_a.at[m], 2 * high + 1 - low)
+
+    def stage_b(m, copy):
+        total, keep, _, arrived, out, into, _ = bundle(m)
+        copy.wait()
+        keep[...] = total[:, part_of(low, 2 * quarter), :] + arrived[...].astype(f32)
+        out[...] = keep[:, part_of(1 - high, quarter), :].astype(b16)
+        return swap(out, into, ssem_b.at[m], rsem_b.at[m], 2 * (1 - high) + low)
+
+    def stage_c(m, copy):
+        _, keep, _, _, _, arrived, _ = bundle(m)
+        copy.wait()
+        mine = (keep[:, part_of(high, quarter), :] + arrived[...].astype(f32)).astype(b16)
+        if m == 3:
+            full_f[slot] = mine[0]
+            return None
+        send_c[m] = mine
+        copies = []
+        for r in range(1, peers):
+            p = lax.rem(me + r, peers)
+            copies.append(
+                pltpu.make_async_remote_copy(
+                    src_ref=send_c.at[m, p],
+                    dst_ref=recv_c.at[m, me],
+                    send_sem=ssem_c.at[m, r],
+                    recv_sem=rsem_c.at[m, r],
+                    device_id={"seq": p},
+                    device_id_type=MESH,
+                )
+            )
+        for c in copies:
+            c.start()
+        recv_c[m, me] = send_c[m, me]
+        return copies
+
+    def stage_d(m, copies):
+        whole = bundle(m)[-1]
+        if m < 3:
+            for c in copies:
+                c.wait()
+            whole[slot] = jnp.sum(recv_c[m].astype(f32), axis=0).astype(b16)
+        return [
+            swap(
+                whole.at[slot], whole.at[slot], ssem_d.at[m, r], rsem_d.at[m, r],
+                lax.rem(seat + r, batches),
+            )
+            for r in range(1, batches)
+        ]
+
+    def finish(m, copies):
+        for c in copies:
+            c.wait()
+        out = (out_q, out_o, out_v, out_f)[m]
+        out[...] = bundle(m)[-1][...].astype(f32).reshape(out.shape)
+
+    def weight(m, left, right):
+        acc[m] = (matmul(left, right) * scale).reshape(peers, own, half)
+
     first = out1(0)
     ups[:here] = cot[:, :half]
     ups[here:] = matmul(cot[:, half:], flip).astype(b16)
@@ -357,26 +452,45 @@
     r1, s1 = times(vspec[own:, :], gspec[own:, :], True)
     yspec[:own, :length] = (r0 + r1).astype(b16)
     yspec[:own, length:] = (s0 + s1).astype(b16)
-    grad_f[...] = matmul_t(yspec[:own, :], table[...]) * (scale / length)
+    acc_f[0] = matmul_t(yspec[:own, :], table[...]) * (scale / length)
+    af = stage_a(3)
 
     for c in third:
         c.wait()
     conv = jnp.concatenate([recv2[0].T, recv2[1].T], axis=0).astype(f32)
+    grad_query = (gates[...].astype(f32) * conv).astype(b16)
+    weight(0, strands_t[...], grad_query)
+    a0 = stage_a(0)
     gated = (query[...].astype(f32) * conv).astype(b16)
-    grad_query = (gates[...].astype(f32) * conv).astype(b16)
-    grad_w[:, :half] = (matmul(strands_t[...], grad_query) * scale).astype(grad_w.dtype)
-    grad_w[:, 2 * half :] = (matmul(gated.T, ups[...]) * scale).astype(grad_w.dtype)
+    weight(1, gated.T, ups[...])
+    a1 = stage_a(1)
+    bf = stage_b(3, af)
     total = strands[...].astype(f32) + matmul(gated, wo[...])
     block[:, :half] = total[:here].astype(b16)
     block[:, half:] = matmul(total[here:].astype(b16), flip).astype(b16)
-    total = ups[...].astype(f32) + matmul_t(grad_query, wq[...])
+    b0 = stage_b(0, a0)
+    b1 = stage_b(1, a1)
     for c in fourth:
         c.wait()
     grad_value = jnp.concatenate([recv2[2].T, recv2[3].T], axis=0)
-    grad_w[:, half : 2 * half] = (matmul(strands_t[...], grad_value) * scale).astype(grad_w.dtype)
-    total = total + matmul_t(grad_value, wv[...])
+    weight(2, strands_t[...], grad_value)
+    a2 = stage_a(2)
+    c0 = stage_c(0, b0)
+    c1 = stage_c(1, b1)
+    b2 = stage_b(2, a2)
+    stage_c(3, bf)
+    df = stage_d(3, None)
+    total = ups[...].astype(f32) + matmul_t(grad_query, wq[...]) + matmul_t(grad_value, wv[...])
     grad_tok[:, :half] = total[:here].astype(b16)
     grad_tok[:, half:] = matmul(total[here:].astype(b16), flip).astype(b16)
+    c2 = stage_c(2, b2)
+    d0 = stage_d(0, c0)
+    d1 = stage_d(1, c1)
+    d2 = stage_d(2, c2)
+    finish(3, df)
+    finish(0, d0)
+    finish(1, d1)
+    finish(2, d2)
 
 
 def short_body(tokens, w_query, w_value, w_out, long_filter, cotangent):
@@ -389,16 +503,21 @@
     scale = (2.0 * lax.axis_size("batch") * length) ** (-0.5)
     coarse, fine = angle_parts(length)
     dma = pltpu.SemaphoreType.DMA
-    block, grad_tok, grad_w, grad_f = pl.pallas_call(
+    batches = lax.axis_size("batch")
+    quarter = own // batches
+    vmem = pltpu.VMEM
+    block, grad_tok, *sums = pl.pallas_call(
         functools.partial(fused, peers, scale),
         out_shape=(
             jax.ShapeDtypeStruct((here, 2 * half), b16),
             jax.ShapeDtypeStruct((here, 2 * half), b16),
-            jax.ShapeDtypeStruct((half, 3 * half), b16),
+            jax.ShapeDtypeStruct((own, half), f32),
+            jax.ShapeDtypeStruct((own, half), f32),
+            jax.ShapeDtypeStruct((own, half), f32),
             jax.ShapeDtypeStruct((own, length), f32),
         ),
         in_specs=[pl.BlockSpec(memory_space=pltpu.VMEM)] * 8,
-        out_specs=(pl.BlockSpec(memory_space=pltpu.VMEM),) * 4,
+        out_specs=(pl.BlockSpec(memory_space=pltpu.VMEM),) * 6,
         scratch_shapes=[
             pltpu.VMEM((length, 2 * length), b16),
             pltpu.VMEM((2 * here, half), b16),
@@ -420,30 +539,46 @@
             dma((2, peers)),
             dma((2, peers)),
             dma((2,)),
+            vmem((3, peers, own, half), f32),
+            vmem((3, peers, 2 * quarter, half), f32),
+            vmem((3, peers, 2 * quarter, half), b16),
+            vmem((3, peers, 2 * quarter, half), b16),
+            vmem((3, peers, quarter, half), b16),
+            vmem((3, peers, quarter, half), b16),
+            vmem((3, peers, quarter, half), b16),
+            vmem((3, peers, quarter, half), b16),
+            vmem((3, batches, quarter, half), b16),
+            vmem((1, own, length), f32),
+            vmem((1, 2 * quarter, length), f32),
+            vmem((1, 2 * quarter, length), b16),
+            vmem((1, 2 * quarter, length), b16),
+            vmem((1, quarter, length), b16),
+            vmem((1, quarter, length), b16),
+            vmem((batches, quarter, length), b16),
+            dma((4,)),
+            dma((4,)),
+            dma((4,)),
+            dma((4,)),
+            dma((3, peers)),
+            dma((3, peers)),
+            dma((4, batches)),
+            dma((4, batches)),
         ],
         compiler_params=pltpu.CompilerParams(
             collective_id=0, has_side_effects=True, vmem_limit_bytes=60 << 20
         ),
     )(tokens[0], w_query, w_value, w_out, long_filter, cotangent[0], coarse, fine)
-    share = lax.psum_scatter(grad_w, "seq", scatter_dimension=0, tiled=True)
-    share = lax.psum(share, "batch").astype(f32)
-    total_f = lax.psum(grad_f.astype(b16), "batch").astype(f32)
-    return (
-        block[None],
-        grad_tok[None],
-        share[:, :half],
-        share[:, half : 2 * half],
-        share[:, 2 * half :],
-        total_f,
-    )
-
-
-def fits(tokens, peers):
-    return (tokens.shape[1] * peers) ** 2 * 4 <= 8 << 20
+    return (block[None], grad_tok[None], *sums)
+
+
+def fits(tokens, half):
+    peers, batches = lax.axis_size("seq"), lax.axis_size("batch")
+    small = (tokens.shape[1] * peers) ** 2 * 4 <= 8 << 20
+    return small and batches == 4 and half % (16 * batches * peers) == 0
 
 
 def choose(tokens, *rest):
-    short = fits(tokens, lax.axis_size("seq"))
+    short = fits(tokens, rest[0].shape[0])
     return (short_body if short else body)(tokens, *rest)
 
 

time: 153 us -> 61.6 us (0.40)
  waiting for transfers between devices: 98.7 us -> 0 us
  Pallas kernels: 33.8 us -> 55.1 us
  between operations: 14.1 us -> 0.66 us
  other arithmetic: 2.29 us -> 0 us
  local copies, waits for them, and re-layouts: 3.92 us -> 5.68 us
    reduce_scatter x1 -> x0, waiting for transfers between devices: 64.2 us -> none  [short_body(): share = lax.psum_scatter(grad_w, 'seq', scatter_dimension=0, tiled=True)]
    psum x1 -> x0, waiting for transfers between devices: 34.4 us -> none  [short_body(): share = lax.psum(share, 'batch').astype(f32)]
    pallas_call x1, Pallas kernels: 33.8 us -> 55.1 us  [short_body(): pl.pallas_call(functools.partial(fused, peers, scale), out_shape=(jax.Sha...]
    unnamed x8 -> x16, local copies, waits for them, and re-layouts: 2.26 us -> 5.68 us
    convert_element_type x2 -> x0, other arithmetic: 2.29 us -> none  [short_body(): total_f = lax.psum(grad_f.astype(b16), 'batch').astype(f32)]
    slice x1 -> x0, local copies, waits for them, and re-layouts: 1.65 us -> none  [short_body(): share[:, 2 * half:]]
  transfers between devices with their start and end apart: 2 -> 0, of which waited for: 2 -> 0; matrix products, arithmetic and copies ran while one was open for 0% -> 0% of each run, Pallas kernels for 0% -> 0%
where the time goes in v2:
time: 61.6 us; the launch traced here: 61.4 us
  Pallas kernels  55.1 us (89%)
  local copies, waits for them, and re-layouts  5.68 us (9%)
  between operations  0.66 us (1%)
    pallas_call x1, Pallas kernels, short_body(): pl.pallas_call(functools.partial(fused, peers, scale), out_shape=(jax.Sha...  55.1 us
    unnamed x16, local copies, waits for them, and re-layouts  5.68 us

profile of v2, /device:TPU:0, one launch (start us, length us, event | category | flops | bytes accessed | tf_op | source)
XLA Modules:
  0.0 61.4 jit_solution(312282180224703039)
XLA Ops:
  0.6 55.1 %shard_map.127 = (bf16[128,1024]{1,0:T(8,128)(2,1)}, bf16[128,1024]{1,0:T(8,128)(2,1)}, f32[64,512]{1,0:T(8,128)}, f32[64,512]{1,0:T(8,128)}, f32[64,512]{1,0:T(8,128)}, /*index=5*/f32[64,1024]{1,0:T(8,128)}) custom-call(bf16[128,1024]{1,0:T(8,128)(2,1)} %bitcast.6, bf16[512,512]{1,0:T(8,128)(2,1)} %wq.1, bf16[512,512]{1,0:T(8,128)(2,1)} %wv.1, ...), custom_call_target="tpu_custom_call" | custom-call | tf_op jit(solution)/shard_map/pallas_call | solution.py:509
  55.7 0.0 copy-start.1
  55.7 1.7 %copy.20 = bf16[1,128,1024]{2,1,0:T(8,128)(2,1)} copy(bf16[1,128,1024]{2,1,0:T(8,128)(2,1)} %bitcast.5) | data formatting | bytes 524288
  57.4 0.0 copy-done.1
  57.4 0.0 copy-start.4
  57.4 0.7 %copy.21 = bf16[1,128,1024]{2,1,0:T(8,128)(2,1)} copy(bf16[1,128,1024]{2,1,0:T(8,128)(2,1)S(1)} %bitcast.4) | data formatting | bytes 524288
  58.1 0.3 copy-done.4
  58.4 0.0 copy-start.3
  58.4 0.0 copy-start.2
  58.4 0.7 %copy.22 = f32[64,512]{1,0:T(8,128)} copy(f32[64,512]{1,0:T(8,128)S(1)} %copy-done.4) | data formatting | bytes 262144
  59.1 0.3 copy-done.3
  59.4 0.0 copy-start
  59.4 0.7 %copy.23 = f32[64,512]{1,0:T(8,128)} copy(f32[64,512]{1,0:T(8,128)S(1)} %copy-done.3) | data formatting | bytes 262144
  60.0 0.0 copy-done.2
  60.0 0.7 %copy.24 = f32[64,512]{1,0:T(8,128)} copy(f32[64,512]{1,0:T(8,128)S(1)} %copy-done.2) | data formatting | bytes 262144
  60.7 0.0 copy-done
  60.7 0.7 %copy.25 = f32[64,1024]{1,0:T(8,128)} copy(f32[64,1024]{1,0:T(8,128)S(1)} %copy-done) | data formatting | bytes 524288
Async XLA Ops:
  55.7 1.7 %copy-start.1 = (bf16[128,1024]{1,0:T(8,128)(2,1)S(1)}, bf16[128,1024]{1,0:T(8,128)(2,1)}, u32[]{:S(2)}) copy-start(bf16[128,1024]{1,0:T(8,128)(2,1)} %get-tuple-element.13) | copy-start | bytes 786436
  57.4 1.0 %copy-start.4 = (f32[64,512]{1,0:T(8,128)S(1)}, f32[64,512]{1,0:T(8,128)}, u32[]{:S(2)}) copy-start(f32[64,512]{1,0:T(8,128)} %get-tuple-element.26) | copy-start | bytes 393220
  58.4 1.0 %copy-start.3 = (f32[64,512]{1,0:T(8,128)S(1)}, f32[64,512]{1,0:T(8,128)}, u32[]{:S(2)}) copy-start(f32[64,512]{1,0:T(8,128)} %get-tuple-element.27) | copy-start | bytes 393220
  58.4 1.6 %copy-start.2 = (f32[64,512]{1,0:T(8,128)S(1)}, f32[64,512]{1,0:T(8,128)}, u32[]{:S(2)}) copy-start(f32[64,512]{1,0:T(8,128)} %get-tuple-element.28) | copy-start | bytes 393220
  59.4 1.3 %copy-start = (f32[64,1024]{1,0:T(8,128)S(1)}, f32[64,1024]{1,0:T(8,128)}, u32[]{:S(2)}) copy-start(f32[64,1024]{1,0:T(8,128)} %get-tuple-element.29) | copy-start | bytes 786436

commit v3 on v2

--- a/solution.py
+++ b/solution.py
@@ -227,8 +227,10 @@
 
 def fused(
     peers, scale,
-    tok, wq, wv, wo, taps, cot, coarse, fine,
-    block, grad_tok, out_q, out_v, out_o, out_f,
+    tok_in, wq_in, wv_in, wo_in, taps_in, cot_in, coarse_in, fine_in,
+    block_out, grad_out, out_w, out_f,
+    block, grad_tok, osem,
+    tok, wq, wv, wo, taps, cot, coarse, fine, lsem,
     table, strands, ups, strands_t, query, gates, send1, recv1, send2, recv2,
     vspec, gspec, hspec, yspec,
     ssem1, rsem1, lsem1, ssem2, rsem2, lsem2,
@@ -236,9 +238,9 @@
     acc_f, kept_f, send_af, recv_af, send_bf, recv_bf, full_f,
     ssem_a, rsem_a, ssem_b, rsem_b, ssem_c, rsem_c, ssem_d, rsem_d,
 ):
-    f32, b16 = jnp.float32, jnp.bfloat16
     me = lax.axis_index("seq")
     here, half = tok.shape[0], wq.shape[0]
+    f32, b16 = jnp.float32, jnp.bfloat16
     own = half // peers
     length = here * peers
 
@@ -253,6 +255,15 @@
         pl.semaphore_signal(
             barrier, inc=1, device_id={"batch": lax.rem(seat + r, batches)}, device_id_type=MESH
         )
+    loads = {}
+    pairs = (
+        ("tok", tok_in, tok), ("wv", wv_in, wv), ("cot", cot_in, cot), ("wo", wo_in, wo),
+        ("wq", wq_in, wq), ("coarse", coarse_in, coarse), ("fine", fine_in, fine),
+        ("taps", taps_in, taps),
+    )
+    for index, (name, src, dst) in enumerate(pairs):
+        loads[name] = pltpu.make_async_copy(src, dst, lsem.at[index])
+        loads[name].start()
     low, high = lax.rem(seat, 2), seat // 2
     quarter = own // batches
     slot = 2 * low + high
@@ -261,11 +272,22 @@
         + lax.broadcasted_iota(jnp.int32, (half, half), 1)
         == half - 1
     ).astype(f32).astype(b16)
+    loads["tok"].wait()
     strands[:here] = tok[:, :half]
     strands[here:] = matmul(tok[:, half:], flip).astype(b16)
+    loads["wv"].wait()
     value = matmul(strands[...], wv[...]).astype(b16)
     send1[0] = value[:here].T
     send1[1] = value[here:].T
+    for name in ("cot", "wo", "wq"):
+        loads[name].wait()
+    ups[:here] = cot[:, :half]
+    ups[here:] = matmul(cot[:, half:], flip).astype(b16)
+    query[...] = matmul(strands[...], wq[...]).astype(b16)
+    gates[...] = matmul_t(ups[...], wo[...]).astype(b16)
+    grad_conv = (gates[...].astype(f32) * query[...].astype(f32)).astype(b16)
+    send1[2] = grad_conv[:here].T
+    send1[3] = grad_conv[here:].T
     pl.semaphore_wait(barrier, peers + batches - 2)
 
     def rows_of(p):
@@ -275,7 +297,7 @@
         return pl.ds(pl.multiple_of(p * here, here), here)
 
     def out1(part):
-        pair = pl.ds(2 * part, 2)
+        pair = pl.ds((0, 2, 3)[part], (2, 1, 1)[part])
         copies = []
         for r in range(1, peers):
             p = lax.rem(me + r, peers)
@@ -299,7 +321,7 @@
         return copies
 
     def out2(part):
-        pair = pl.ds(2 * part, 2)
+        pair = pl.ds((0, 2, 3)[part], (2, 1, 1)[part])
         copies = []
         for r in range(1, peers):
             p = lax.rem(me + r, peers)
@@ -399,21 +421,21 @@
     def finish(m, copies):
         for c in copies:
             c.wait()
-        out = (out_q, out_o, out_v, out_f)[m]
-        out[...] = bundle(m)[-1][...].astype(f32).reshape(out.shape)
+        target = out_f if m == 3 else out_w.at[m]
+        return leave(m, bundle(m)[-1], target)
+
+    def leave(index, src, dst):
+        copy = pltpu.make_async_copy(src, dst, osem.at[index])
+        copy.start()
+        return copy
 
     def weight(m, left, right):
         acc[m] = (matmul(left, right) * scale).reshape(peers, own, half)
 
     first = out1(0)
-    ups[:here] = cot[:, :half]
-    ups[here:] = matmul(cot[:, half:], flip).astype(b16)
-    query[...] = matmul(strands[...], wq[...]).astype(b16)
-    gates[...] = matmul_t(ups[...], wo[...]).astype(b16)
-    grad_conv = (gates[...].astype(f32) * query[...].astype(f32)).astype(b16)
-    send1[2] = grad_conv[:here].T
-    send1[3] = grad_conv[here:].T
     second = out1(1)
+    for name in ("coarse", "fine", "taps"):
+        loads[name].wait()
 
     count, step = coarse.shape[1], fine.shape[1]
 
@@ -427,33 +449,31 @@
     strands_t[...] = strands[...].T
     hspec[...] = matmul(taps[...].astype(b16), table[...])
 
-    def spread(part, causal):
-        spec = (vspec, gspec)[part]
-        for strand in range(2):
-            row = pl.ds(strand * own, own)
-            r, s = times(spec[row, :], hspec[...], strand != causal)
-            yspec[row, :length] = r.astype(b16)
-            yspec[row, length:] = s.astype(b16)
-        back = (matmul_t(yspec[...], table[...]) * (1.0 / length)).astype(b16)
-        send2[2 * part] = back[:own]
-        send2[2 * part + 1] = back[own:]
+    def product(row, spec, conj):
+        r, s = times(spec[row, :], hspec[...], conj)
+        yspec[row, :length] = r.astype(b16)
+        yspec[row, length:] = s.astype(b16)
+
+    def back_value(strand, copies):
+        for c in copies:
+            c.wait()
+        row = pl.ds(strand * own, own)
+        gspec[row, :] = matmul(recv1[2 + strand], table[...])
+        product(row, gspec, strand == 0)
+        send2[2 + strand] = (matmul_t(yspec[row, :], table[...]) * (1.0 / length)).astype(b16)
+        return out2(1 + strand)
 
     for c in first:
         c.wait()
     vspec[...] = matmul(recv1[0:2].reshape(2 * own, length), table[...])
-    spread(0, 0)
+    product(pl.ds(0, own), vspec, False)
+    product(pl.ds(own, own), vspec, True)
+    conv_own = (matmul_t(yspec[...], table[...]) * (1.0 / length)).astype(b16)
+    send2[0] = conv_own[:own]
+    send2[1] = conv_own[own:]
     third = out2(0)
-    for c in second:
-        c.wait()
-    gspec[...] = matmul(recv1[2:4].reshape(2 * own, length), table[...])
-    spread(1, 1)
-    fourth = out2(1)
-    r0, s0 = times(gspec[:own, :], vspec[:own, :], True)
-    r1, s1 = times(vspec[own:, :], gspec[own:, :], True)
-    yspec[:own, :length] = (r0 + r1).astype(b16)
-    yspec[:own, length:] = (s0 + s1).astype(b16)
-    acc_f[0] = matmul_t(yspec[:own, :], table[...]) * (scale / length)
-    af = stage_a(3)
+    late = out1(2)
+    fourth = back_value(0, second)
 
     for c in third:
         c.wait()
@@ -464,33 +484,58 @@
     gated = (query[...].astype(f32) * conv).astype(b16)
     weight(1, gated.T, ups[...])
     a1 = stage_a(1)
-    bf = stage_b(3, af)
+    b0 = stage_b(0, a0)
+    b1 = stage_b(1, a1)
+    fifth = back_value(1, late)
+    r0, s0 = times(gspec[:own, :], vspec[:own, :], True)
+    r1, s1 = times(vspec[own:, :], gspec[own:, :], True)
+    yspec[:own, :length] = (r0 + r1).astype(b16)
+    yspec[:own, length:] = (s0 + s1).astype(b16)
+    acc_f[0] = matmul_t(yspec[:own, :], table[...]) * (scale / length)
+    af = stage_a(3)
     total = strands[...].astype(f32) + matmul(gated, wo[...])
     block[:, :half] = total[:here].astype(b16)
     block[:, half:] = matmul(total[here:].astype(b16), flip).astype(b16)
-    b0 = stage_b(0, a0)
-    b1 = stage_b(1, a1)
+    o4 = leave(4, block, block_out)
+    c0 = stage_c(0, b0)
+    bf = stage_b(3, af)
     for c in fourth:
         c.wait()
-    grad_value = jnp.concatenate([recv2[2].T, recv2[3].T], axis=0)
-    weight(2, strands_t[...], grad_value)
+    value_0 = recv2[2].T
+    early = matmul(strands_t[:, :here], value_0)
+    c1 = stage_c(1, b1)
+    for c in fifth:
+        c.wait()
+    value_1 = recv2[3].T
+    acc[2] = ((early + matmul(strands_t[:, here:], value_1)) * scale).reshape(peers, own, half)
     a2 = stage_a(2)
-    c0 = stage_c(0, b0)
-    c1 = stage_c(1, b1)
+    stage_c(3, bf)
     b2 = stage_b(2, a2)
-    stage_c(3, bf)
-    df = stage_d(3, None)
+    grad_value = jnp.concatenate([value_0, value_1], axis=0)
     total = ups[...].astype(f32) + matmul_t(grad_query, wq[...]) + matmul_t(grad_value, wv[...])
     grad_tok[:, :half] = total[:here].astype(b16)
     grad_tok[:, half:] = matmul(total[here:].astype(b16), flip).astype(b16)
+    o5 = leave(5, grad_tok, grad_out)
     c2 = stage_c(2, b2)
+    df = stage_d(3, None)
     d0 = stage_d(0, c0)
     d1 = stage_d(1, c1)
+    o3 = finish(3, df)
+    o0 = finish(0, d0)
+    o1 = finish(1, d1)
     d2 = stage_d(2, c2)
-    finish(3, df)
-    finish(0, d0)
-    finish(1, d1)
-    finish(2, d2)
+    o2 = finish(2, d2)
+    for c in (o0, o1, o2, o3, o4, o5):
+        c.wait()
+
+
+def emit(block, grad_tok, weights, filters, block_out, grad_out, out_q, out_v, out_o, out_f):
+    block_out[...] = block[...]
+    grad_out[...] = grad_tok[...]
+    out_q[...] = weights[0].reshape(out_q.shape).astype(out_q.dtype)
+    out_o[...] = weights[1].reshape(out_o.shape).astype(out_o.dtype)
+    out_v[...] = weights[2].reshape(out_v.shape).astype(out_v.dtype)
+    out_f[...] = filters[...].reshape(out_f.shape).astype(out_f.dtype)
 
 
 def short_body(tokens, w_query, w_value, w_out, long_filter, cotangent):
@@ -506,19 +551,23 @@
     batches = lax.axis_size("batch")
     quarter = own // batches
     vmem = pltpu.VMEM
-    block, grad_tok, *sums = pl.pallas_call(
+    arguments = (tokens[0], w_query, w_value, w_out, long_filter, cotangent[0], coarse, fine)
+    block, grad_tok, weights, filters = pl.pallas_call(
         functools.partial(fused, peers, scale),
         out_shape=(
             jax.ShapeDtypeStruct((here, 2 * half), b16),
             jax.ShapeDtypeStruct((here, 2 * half), b16),
-            jax.ShapeDtypeStruct((own, half), f32),
-            jax.ShapeDtypeStruct((own, half), f32),
-            jax.ShapeDtypeStruct((own, half), f32),
-            jax.ShapeDtypeStruct((own, length), f32),
+            jax.ShapeDtypeStruct((3, batches, quarter, half), b16),
+            jax.ShapeDtypeStruct((batches, quarter, length), b16),
         ),
-        in_specs=[pl.BlockSpec(memory_space=pltpu.VMEM)] * 8,
-        out_specs=(pl.BlockSpec(memory_space=pltpu.VMEM),) * 6,
+        in_specs=[pl.BlockSpec(memory_space=pltpu.HBM)] * 8,
+        out_specs=(pl.BlockSpec(memory_space=pltpu.HBM),) * 4,
         scratch_shapes=[
+            vmem((here, 2 * half), b16),
+            vmem((here, 2 * half), b16),
+            dma((6,)),
+            *(vmem(a.shape, a.dtype) for a in arguments),
+            dma((8,)),
             pltpu.VMEM((length, 2 * length), b16),
             pltpu.VMEM((2 * here, half), b16),
             pltpu.VMEM((2 * here, half), b16),
@@ -533,12 +582,12 @@
             pltpu.VMEM((2 * own, 2 * length), f32),
             pltpu.VMEM((own, 2 * length), f32),
             pltpu.VMEM((2 * own, 2 * length), b16),
-            dma((2, peers)),
-            dma((2, peers)),
-            dma((2,)),
-            dma((2, peers)),
-            dma((2, peers)),
-            dma((2,)),
+            dma((3, peers)),
+            dma((3, peers)),
+            dma((3,)),
+            dma((3, peers)),
+            dma((3, peers)),
+            dma((3,)),
             vmem((3, peers, own, half), f32),
             vmem((3, peers, 2 * quarter, half), f32),
             vmem((3, peers, 2 * quarter, half), b16),
@@ -565,9 +614,23 @@
             dma((4, batches)),
         ],
         compiler_params=pltpu.CompilerParams(
-            collective_id=0, has_side_effects=True, vmem_limit_bytes=60 << 20
+            collective_id=0, has_side_effects=True, vmem_limit_bytes=65900000
         ),
-    )(tokens[0], w_query, w_value, w_out, long_filter, cotangent[0], coarse, fine)
+    )(*arguments)
+    block, grad_tok, *sums = pl.pallas_call(
+        emit,
+        out_shape=(
+            jax.ShapeDtypeStruct((here, 2 * half), b16),
+            jax.ShapeDtypeStruct((here, 2 * half), b16),
+            jax.ShapeDtypeStruct((own, half), f32),
+            jax.ShapeDtypeStruct((own, half), f32),
+            jax.ShapeDtypeStruct((own, half), f32),
+            jax.ShapeDtypeStruct((own, length), f32),
+        ),
+        in_specs=[pl.BlockSpec(memory_space=pltpu.VMEM)] * 4,
+        out_specs=(pl.BlockSpec(memory_space=pltpu.VMEM),) * 6,
+        compiler_params=pltpu.CompilerParams(vmem_limit_bytes=65900000),
+    )(block, grad_tok, weights, filters)
     return (block[None], grad_tok[None], *sums)
 
 

time: 61.6 us -> 56.4 us (0.916)
  local copies, waits for them, and re-layouts: 5.68 us -> 0 us
    unnamed x16 -> x0, local copies, waits for them, and re-layouts: 5.68 us -> none
    pallas_call x0 -> x1, Pallas kernels: none -> 2.15 us  [short_body(): pl.pallas_call(emit, out_shape=(jax.ShapeDtypeStruct((here, 2 * half), b1...]
    pallas_call x1, Pallas kernels: 55.1 us -> 53.5 us  [short_body(): pl.pallas_call(functools.partial(fused, peers, scale), out_shape=(jax.Sha...]
where the time goes in v3:
time: 56.4 us; the launch traced here: 56.2 us
  Pallas kernels  55.6 us (99%)
  between operations  0.64 us (1%)
    pallas_call x1, Pallas kernels, short_body(): pl.pallas_call(functools.partial(fused, peers, scale), out_shape=(jax.Sha...  53.5 us
    pallas_call x1, Pallas kernels, short_body(): pl.pallas_call(emit, out_shape=(jax.ShapeDtypeStruct((here, 2 * half), b1...  2.15 us

profile of v3, /device:TPU:0, one launch (start us, length us, event | category | flops | bytes accessed | tf_op | source)
XLA Modules:
  0.0 56.2 jit_solution(2691083928115389029)
XLA Ops:
  0.6 53.5 %shard_map.127 = (bf16[128,1024]{1,0:T(8,128)(2,1)}, bf16[128,1024]{1,0:T(8,128)(2,1)}, bf16[3,4,16,512]{3,2,1,0:T(8,128)(2,1)}, bf16[4,16,1024]{2,1,0:T(8,128)(2,1)}) custom-call(bf16[128,1024]{1,0:T(8,128)(2,1)} %bitcast.4, bf16[512,512]{1,0:T(8,128)(2,1)} %wq_in.1, bf16[512,512]{1,0:T(8,128)(2,1)} %wv_in.1, bf16[512,512]{1,0:T(8,128)(2,1)} %wo_in.1, ...), custom_call_target="tpu_custom_call" | custom-call | tf_op jit(solution)/shard_map/pallas_call | solution.py:555
  54.1 2.1 %shard_map.128 = (bf16[128,1024]{1,0:T(8,128)(2,1)}, bf16[128,1024]{1,0:T(8,128)(2,1)}, f32[64,512]{1,0:T(8,128)}, f32[64,512]{1,0:T(8,128)}, f32[64,512]{1,0:T(8,128)}, /*index=5*/f32[64,1024]{1,0:T(8,128)}) custom-call(bf16[128,1024]{1,0:T(8,128)(2,1)} %get-tuple-element.16.block, bf16[128,1024]{1,0:T(8,128)(2,1)} %get-tuple-element.17.grad_tok, ...), custom_call_target="tpu_custom_call" | custom-call | tf_op jit(solution)/shard_map/pallas_call | solution.py:620
